TPU v7x, 256 devices: a whole 4x4x8 slice. The times are simulated.
256 devices in a mesh: fx: 32 (over z, x), fy: 8 (over y, core).
Axes of the slice: x: 4, y: 4, z: 8, core: 2. Of those that a mesh axis runs over, the one named last changes fastest.
Arguments:
- right_side: float32 [4096, 2048], P(('fx', 'fy'))
- coupling: float32 [4096, 11, 4096], P(('fx', 'fy')), may hold values from -0.109375 to 0.109375
- face_columns: int32 [4096, 11], P(('fx', 'fy')), may hold values from 0 to 31, as said below
- ghost_lists: int32 [1024, 4], P(('fx', 'fy')), may hold values from 0 to 15, as said below
Outputs:
- solution: float32 [4096, 2048], P(('fx', 'fy'))
- residual: float32 [4096, 2048], P(('fx', 'fy'))
Inputs may be any that keep to these rules, and one draw needn't show every extreme that they name: face_columns[f, 0] is f's own index within its block; entries 1 to 6 name other faces of the same block, all distinct and below 16; entries 7 to 10 are distinct and name received faces, 16 + d * 4 + g for the g-th face of group d of the extended list; every received slot of every block is named by some row of that block. `ghost_lists`: each row names 4 distinct faces of its block by local index.
All inputs are finite; a program needn't handle non-finite values.
Results may differ from a plain program's by a relative error of at most 0.0003.
Values sent between devices are 32-bit elements; how exact they have to be, the bound alone decides.
No kernel may reach another device: no remote copies, remote signals or barrier semaphores. Data moves between devices by JAX's collectives and lax.ppermute only.
A program may use at most 64 MiB of HBM per device.

v0:
```python
import jax
import jax.numpy as jnp
from jax import lax
from jax.sharding import PartitionSpec as P

DOF = 64
NRHS = 32
BLOCKS = 11
POWERS = 3


def from_behind(block, axis, distance):
    devices = range(lax.axis_size(axis))
    route = [(i - distance, i) for i in devices if i - distance in devices]
    return lax.ppermute(block, axis, route)


def receive_rows(field, ghost_lists):
    from_lower_x = from_behind(jnp.take(field, ghost_lists[1], axis=0), "fx", 1)
    from_upper_x = from_behind(jnp.take(field, ghost_lists[0], axis=0), "fx", -1)
    from_lower_y = from_behind(jnp.take(field, ghost_lists[3], axis=0), "fy", 1)
    from_upper_y = from_behind(jnp.take(field, ghost_lists[2], axis=0), "fy", -1)
    return jnp.concatenate([from_lower_x, from_upper_x, from_lower_y, from_upper_y], axis=0)


def contract(block_mats, picked):
    face_count = picked.shape[0]
    shaped = picked.reshape(face_count, picked.shape[1], DOF, NRHS)
    result = jnp.einsum("fkab,fkbr->far", block_mats, shaped, precision=lax.Precision.HIGHEST)
    return result.reshape(face_count, DOF * NRHS)


def solve_small(gram_total):
    count = NRHS
    row_ids = jnp.arange((POWERS + 1) * count)[:, None]
    col_ids = jnp.arange(POWERS * count)[None, :]
    shift_map = ((row_ids == col_ids) | (row_ids == col_ids + count)).astype(jnp.float32)
    first = (row_ids == jnp.arange(count)[None, :]).astype(jnp.float32)
    high = lax.Precision.HIGHEST
    normal_matrix = jnp.dot(
        shift_map.T, jnp.dot(gram_total, shift_map, precision=high), precision=high
    )
    right_terms = jnp.dot(shift_map.T, gram_total[:, :count], precision=high)
    factor = jnp.linalg.cholesky(normal_matrix)
    coeffs = jax.scipy.linalg.cho_solve((factor, True), right_terms)
    combo = first - jnp.dot(shift_map, coeffs, precision=high)
    return (coeffs, combo)


def on_device(right_side, coupling, face_columns, ghost_lists):
    face_count = right_side.shape[0]
    block_mats = coupling.reshape(face_count, BLOCKS, DOF, DOF)
    high = lax.Precision.HIGHEST

    def as_rows(field):
        return field.reshape(face_count * DOF, NRHS)

    fields = [right_side]
    for power_index in range(POWERS):
        power_field = fields[-1]
        received = receive_rows(power_field, ghost_lists)
        extended = jnp.concatenate([power_field, received], axis=0)
        fields.append(contract(block_mats, jnp.take(extended, face_columns, axis=0)))
    stacked = jnp.concatenate([as_rows(item) for item in fields], axis=1)
    local_gram = jnp.dot(stacked.T, stacked, precision=high, preferred_element_type=jnp.float32)
    gram_total = lax.psum(local_gram, ("fx", "fy"))
    coeffs, combo = solve_small(gram_total)
    solution = jnp.dot(stacked[:, : POWERS * NRHS], coeffs, precision=high)
    residual = jnp.dot(stacked, combo, precision=high)
    return (solution.reshape(face_count, DOF * NRHS), residual.reshape(face_count, DOF * NRHS))


def solution(mesh):
    placed = (
        P(("fx", "fy"), None),
        P(("fx", "fy"), None, None),
        P(("fx", "fy"), None),
        P(("fx", "fy"), None),
    )
    return jax.shard_map(
        on_device,
        mesh=mesh,
        in_specs=placed,
        out_specs=(P(("fx", "fy"), None), P(("fx", "fy"), None)),
        check_vma=False,
    )
```

profile of v0, /device:TPU:1, one launch (start us, length us, event | category | flops | bytes accessed | tf_op | source)
XLA Modules:
  0.0 415.1 jit_solution(4617153673329050650)
XLA Ops:
  9.6 3.9 collective-permute-start
  18.0 4.0 collective-permute-start.2
  23.7 1.9 collective-permute-start.3
  27.1 5.7 %reshape.61 = f32[16,11,64,64]{3,2,0,1:T(8,128)} reshape(f32[16,11,4096]{2,0,1:T(8,128)} %param.9) | data formatting | bytes 5767168 | tf_op jit(solution)/shard_map/reshape | solution.py:52
  35.6 1.8 broadcast_select_fusion.2
  37.4 3.6 reshape.245
  41.0 12.0 %fusion.6 = f32[16,64,32]{1,2,0:T(8,128)S(1)} fusion(f32[16,11,64,64]{3,2,0,1:T(8,128)} %reshape.61, f32[16,11,64,32]{3,2,1,0:T(8,128)} %reshape.245), kind=kOutput, calls=%fused_computation.21 | convolution fusion | flops 276824064 | bytes 4456448 | tf_op jit(solution)/shard_map/fkab,fkbr->far/dot_general | solution.py:29
  57.2 3.6 collective-permute-start.6
  60.9 1.9 collective-permute-start.7
  62.9 5.1 %collective-permute-start.4 = (f32[4,2048]{1,0:T(4,128)S(1)}, f32[4,2048]{1,0:T(4,128)S(1)}, u32[]{:S(2)}, u32[]{:S(2)}) collective-permute-start(f32[4,2048]{1,0:T(4,128)S(1)} %broadcast_select_fusion.10), channel_id=1, source_target_pairs={{0,8},{8,16},{16,24},{24,32},{32,40},{40,48},{48,56},{56,64},{64,7... | collective-permute-start | bytes 98312 | tf_op jit(solution)/shard_map/ppermute | solution.py:15
  70.0 1.6 reshape.229
  71.7 3.2 broadcast_select_fusion.1
  74.9 5.2 %reshape.246 = f32[16,11,64,32]{3,2,1,0:T(8,128)} reshape(f32[16,11,2048]{2,1,0:T(8,128)} %broadcast_select_fusion.1) | data formatting | bytes 2883584 | tf_op jit(solution)/shard_map/reshape | solution.py:28
  80.1 12.0 %fusion.9 = f32[16,64,32]{1,2,0:T(8,128)S(1)} fusion(f32[16,11,64,64]{3,2,0,1:T(8,128)} %reshape.61, f32[16,11,64,32]{3,2,1,0:T(8,128)} %reshape.246), kind=kOutput, calls=%fused_computation.22 | convolution fusion | flops 276824064 | bytes 4456448 | tf_op jit(solution)/shard_map/fkab,fkbr->far/dot_general | solution.py:29
  94.9 4.5 %collective-permute-start.10 = (f32[4,2048]{1,0:T(4,128)S(1)}, f32[4,2048]{1,0:T(4,128)S(1)}, u32[]{:S(2)}, u32[]{:S(2)}) collective-permute-start(f32[4,2048]{1,0:T(4,128)S(1)} %broadcast_select_fusion.4), channel_id=1, source_target_pairs={{0,1},{1,2},{2,3},{3,4},{4,5},{5,6},{6,7},{8,9},{9,10},{10,11},{11... | collective-permute-start | bytes 98312 | tf_op jit(solution)/shard_map/ppermute | solution.py:15
  99.5 1.9 collective-permute-start.11
  102.9 4.8 %collective-permute-start.8 = (f32[4,2048]{1,0:T(4,128)S(1)}, f32[4,2048]{1,0:T(4,128)S(1)}, u32[]{:S(2)}, u32[]{:S(2)}) collective-permute-start(f32[4,2048]{1,0:T(4,128)S(1)} %broadcast_select_fusion.6), channel_id=1, source_target_pairs={{0,8},{8,16},{16,24},{24,32},{32,40},{40,48},{48,56},{56,64},{64,7... | collective-permute-start | bytes 98312 | tf_op jit(solution)/shard_map/ppermute | solution.py:15
  111.3 3.2 broadcast_select_fusion
  114.6 5.2 %reshape.247 = f32[16,11,64,32]{3,2,1,0:T(8,128)} reshape(f32[16,11,2048]{2,1,0:T(8,128)} %broadcast_select_fusion) | data formatting | bytes 2883584 | tf_op jit(solution)/shard_map/reshape | solution.py:28
  119.7 12.3 %fusion.12 = f32[16,64,32]{1,2,0:T(8,128)S(1)} fusion(f32[16,11,64,64]{3,2,0,1:T(8,128)} %reshape.61, f32[16,11,64,32]{3,2,1,0:T(8,128)} %reshape.247), kind=kOutput, calls=%fused_computation.23 | convolution fusion | flops 276824064 | bytes 4456448 | tf_op jit(solution)/shard_map/fkab,fkbr->far/dot_general | solution.py:29
  132.7 1.6 fusion.37
  134.4 250.2 %all-reduce.2.cloned.1.call-done = f32[128,128]{1,0:T(8,128)} async-done(((f32[128,128]{1,0:T(8,128)}), f32[128,128]{1,0:T(8,128)}) %all-reduce.2.cloned.1.call-update) | async-done | bytes 65552 | tf_op jit(solution)/shard_map/psum | solution.py:66
  385.9 8.8 %cholesky.16 = f32[96,96]{1,0:T(8,128)S(1)} custom-call(f32[96,96]{1,0:T(8,128)S(1)} %fusion.29), custom_call_target="Cholesky" | custom-call | tf_op jit(solution)/shard_map/jit(cholesky)/cholesky | solution.py:44
  396.1 7.4 %custom-call.10 = f32[1,96,96]{1,2,0:T(8,128)S(1)} custom-call(f32[1,96,96]{2,1,0:T(8,128)S(1)} %fusion.24), custom_call_target="InvertDiagBlocksLowerTriangular" | custom-call | tf_op jit(solution)/shard_map/jit(_cho_solve)/triangular_solve | solution.py:45
  (83 shorter events, 35.3 us)
Async XLA Ops:
  7.2 377.4 %all-reduce.2.cloned.1.call-start = ((), (), s32[]{:S(2)}) async-start(), calls=%async_computation | async-start | bytes 131072 | tf_op jit(solution)/shard_map/psum | solution.py:66
  9.6 23.2 %collective-permute-start = (f32[4,2048]{1,0:T(4,128)S(1)}, f32[4,2048]{1,0:T(4,128)S(1)}, u32[]{:S(2)}, u32[]{:S(2)}) collective-permute-start(f32[4,2048]{1,0:T(4,128)S(1)} %broadcast_select_fusion.14), channel_id=1, source_target_pairs={{0,8},{8,16},{16,24},{24,32},{32,40},{40,48},{48,56},{56,64},{64,7... | collective-permute-start | bytes 98312 | tf_op jit(solution)/shard_map/ppermute | solution.py:15
  15.2 17.6 %collective-permute-start.1 = (f32[4,2048]{1,0:T(4,128)S(1)}, f32[4,2048]{1,0:T(4,128)S(1)}, u32[]{:S(2)}, u32[]{:S(2)}) collective-permute-start(f32[4,2048]{1,0:T(4,128)S(1)} %broadcast_select_fusion.13), channel_id=1, source_target_pairs={{8,0},{16,8},{24,16},{32,24},{40,32},{48,40},{56,48},{64,56},{72,6... | collective-permute-start | bytes 98312 | tf_op jit(solution)/shard_map/ppermute | solution.py:15
  18.0 14.8 %collective-permute-start.2 = (f32[4,2048]{1,0:T(4,128)S(1)}, f32[4,2048]{1,0:T(4,128)S(1)}, u32[]{:S(2)}, u32[]{:S(2)}) collective-permute-start(f32[4,2048]{1,0:T(4,128)S(1)} %broadcast_select_fusion.12), channel_id=1, source_target_pairs={{0,1},{1,2},{2,3},{3,4},{4,5},{5,6},{6,7},{8,9},{9,10},{10,11},{11... | collective-permute-start | bytes 98312 | tf_op jit(solution)/shard_map/ppermute | solution.py:15
  23.7 9.2 %collective-permute-start.3 = (f32[4,2048]{1,0:T(4,128)S(1)}, f32[4,2048]{1,0:T(4,128)S(1)}, u32[]{:S(2)}, u32[]{:S(2)}) collective-permute-start(f32[4,2048]{1,0:T(4,128)S(1)} %broadcast_select_fusion.11), channel_id=1, source_target_pairs={{1,0},{2,1},{3,2},{4,3},{5,4},{6,5},{7,6},{9,8},{10,9},{11,10},{12... | collective-permute-start | bytes 98312 | tf_op jit(solution)/shard_map/ppermute | solution.py:15
  27.1 5.7 %copy-start = (f32[16,2048]{1,0:T(8,128)S(1)}, f32[16,2048]{1,0:T(8,128)}, u32[]{:S(2)}) copy-start(f32[16,2048]{1,0:T(8,128)} %param.8) | copy-start | bytes 393220
  55.8 12.2 %collective-permute-start.5 = (f32[4,2048]{1,0:T(4,128)S(1)}, f32[4,2048]{1,0:T(4,128)S(1)}, u32[]{:S(2)}, u32[]{:S(2)}) collective-permute-start(f32[4,2048]{1,0:T(4,128)S(1)} %broadcast_select_fusion.9), channel_id=1, source_target_pairs={{8,0},{16,8},{24,16},{32,24},{40,32},{48,40},{56,48},{64,56},{72,6... | collective-permute-start | bytes 98312 | tf_op jit(solution)/shard_map/ppermute | solution.py:15
  57.2 10.8 %collective-permute-start.6 = (f32[4,2048]{1,0:T(4,128)S(1)}, f32[4,2048]{1,0:T(4,128)S(1)}, u32[]{:S(2)}, u32[]{:S(2)}) collective-permute-start(f32[4,2048]{1,0:T(4,128)S(1)} %broadcast_select_fusion.8), channel_id=1, source_target_pairs={{0,1},{1,2},{2,3},{3,4},{4,5},{5,6},{6,7},{8,9},{9,10},{10,11},{11... | collective-permute-start | bytes 98312 | tf_op jit(solution)/shard_map/ppermute | solution.py:15
  60.9 7.1 %collective-permute-start.7 = (f32[4,2048]{1,0:T(4,128)S(1)}, f32[4,2048]{1,0:T(4,128)S(1)}, u32[]{:S(2)}, u32[]{:S(2)}) collective-permute-start(f32[4,2048]{1,0:T(4,128)S(1)} %broadcast_select_fusion.7), channel_id=1, source_target_pairs={{1,0},{2,1},{3,2},{4,3},{5,4},{6,5},{7,6},{9,8},{10,9},{11,10},{12... | collective-permute-start | bytes 98312 | tf_op jit(solution)/shard_map/ppermute | solution.py:15
  62.9 5.9 %collective-permute-start.4 = (f32[4,2048]{1,0:T(4,128)S(1)}, f32[4,2048]{1,0:T(4,128)S(1)}, u32[]{:S(2)}, u32[]{:S(2)}) collective-permute-start(f32[4,2048]{1,0:T(4,128)S(1)} %broadcast_select_fusion.10), channel_id=1, source_target_pairs={{0,8},{8,16},{16,24},{24,32},{32,40},{40,48},{48,56},{56,64},{64,7... | collective-permute-start | bytes 98312 | tf_op jit(solution)/shard_map/ppermute | solution.py:15
  94.9 12.9 %collective-permute-start.10 = (f32[4,2048]{1,0:T(4,128)S(1)}, f32[4,2048]{1,0:T(4,128)S(1)}, u32[]{:S(2)}, u32[]{:S(2)}) collective-permute-start(f32[4,2048]{1,0:T(4,128)S(1)} %broadcast_select_fusion.4), channel_id=1, source_target_pairs={{0,1},{1,2},{2,3},{3,4},{4,5},{5,6},{6,7},{8,9},{9,10},{10,11},{11... | collective-permute-start | bytes 98312 | tf_op jit(solution)/shard_map/ppermute | solution.py:15
  99.5 8.3 %collective-permute-start.11 = (f32[4,2048]{1,0:T(4,128)S(1)}, f32[4,2048]{1,0:T(4,128)S(1)}, u32[]{:S(2)}, u32[]{:S(2)}) collective-permute-start(f32[4,2048]{1,0:T(4,128)S(1)} %broadcast_select_fusion.3), channel_id=1, source_target_pairs={{1,0},{2,1},{3,2},{4,3},{5,4},{6,5},{7,6},{9,8},{10,9},{11,10},{12... | collective-permute-start | bytes 98312 | tf_op jit(solution)/shard_map/ppermute | solution.py:15
  101.5 6.3 %collective-permute-start.9 = (f32[4,2048]{1,0:T(4,128)S(1)}, f32[4,2048]{1,0:T(4,128)S(1)}, u32[]{:S(2)}, u32[]{:S(2)}) collective-permute-start(f32[4,2048]{1,0:T(4,128)S(1)} %broadcast_select_fusion.5), channel_id=1, source_target_pairs={{8,0},{16,8},{24,16},{32,24},{40,32},{48,40},{56,48},{64,56},{72,6... | collective-permute-start | bytes 98312 | tf_op jit(solution)/shard_map/ppermute | solution.py:15
  102.9 5.6 %collective-permute-start.8 = (f32[4,2048]{1,0:T(4,128)S(1)}, f32[4,2048]{1,0:T(4,128)S(1)}, u32[]{:S(2)}, u32[]{:S(2)}) collective-permute-start(f32[4,2048]{1,0:T(4,128)S(1)} %broadcast_select_fusion.6), channel_id=1, source_target_pairs={{0,8},{8,16},{16,24},{24,32},{32,40},{40,48},{48,56},{56,64},{64,7... | collective-permute-start | bytes 98312 | tf_op jit(solution)/shard_map/ppermute | solution.py:15
Sparse Core Ops, SparseCore 0:
  134.5 250.0 all-reduce.1
where the time goes:
time: 416 us; the launch traced here: 415 us
  waiting for transfers between devices  252 us (61%)
  matrix products  42.2 us (10%)
  local copies, waits for them, and re-layouts  41.9 us (10%)
  starting transfers between devices  35.5 us (9%)
  other arithmetic  29.4 us (7%)
  between operations  14.5 us (3%)
    psum x1, waiting for transfers between devices, on_device(): gram_total = lax.psum(local_gram, ('fx', 'fy'))  250 us
    dot_general x3, matrix products, contract(): jnp.einsum('fkab,fkbr->far', block_mats, shaped, precision=lax.Precision....  36.3 us
    ppermute x12, starting transfers between devices, from_behind(): return lax.ppermute(block, axis, route)  35.5 us
    reshape x3, local copies, waits for them, and re-layouts, contract(): shaped = picked.reshape(face_count, picked.shape[1], DOF, NRHS)  13.9 us
    another operation x3, other arithmetic, solve_small(): factor = jnp.linalg.cholesky(normal_matrix)  9.45 us
    select_n x4, other arithmetic, on_device(): jnp.take(extended, face_columns, axis=0)  8.94 us
  transfers between devices with their start and end apart: 13, of which 3 were waited for; matrix products, arithmetic and copies ran while one was open for 3% of the time, Pallas kernels for 0%

commit v1 on v0

--- a/solution.py
+++ b/solution.py
@@ -63,7 +63,7 @@
         fields.append(contract(block_mats, jnp.take(extended, face_columns, axis=0)))
     stacked = jnp.concatenate([as_rows(item) for item in fields], axis=1)
     local_gram = jnp.dot(stacked.T, stacked, precision=high, preferred_element_type=jnp.float32)
-    gram_total = lax.psum(local_gram, ("fx", "fy"))
+    gram_total = lax.psum(lax.psum(local_gram, "fy"), "fx")
     coeffs, combo = solve_small(gram_total)
     solution = jnp.dot(stacked[:, : POWERS * NRHS], coeffs, precision=high)
     residual = jnp.dot(stacked, combo, precision=high)

time: 416 us -> 383 us (0.921)
  waiting for transfers between devices: 252 us -> 215 us
    psum x1 -> x2, waiting for transfers between devices: 250 us -> 214 us  [on_device(): gram_total = lax.psum(lax.psum(local_gram, 'fy'), 'fx')]
  transfers between devices with their start and end apart: 13 -> 14, of which waited for: 3 -> 4; matrix products, arithmetic and copies ran while one was open for 3% -> 3% of each run, Pallas kernels for 0% -> 0%
where the time goes in v1:
time: 383 us; the launch traced here: 379 us
  waiting for transfers between devices  215 us (56%)
  matrix products  42 us (11%)
  local copies, waits for them, and re-layouts  41.9 us (11%)
  starting transfers between devices  35.8 us (9%)
  other arithmetic  29.4 us (8%)
  between operations  14.5 us (4%)
    psum x2, waiting for transfers between devices, on_device(): gram_total = lax.psum(lax.psum(local_gram, 'fy'), 'fx')  214 us
    dot_general x3, matrix products, contract(): jnp.einsum('fkab,fkbr->far', block_mats, shaped, precision=lax.Precision....  36 us
    ppermute x12, starting transfers between devices, from_behind(): return lax.ppermute(block, axis, route)  35.5 us
    reshape x3, local copies, waits for them, and re-layouts, contract(): shaped = picked.reshape(face_count, picked.shape[1], DOF, NRHS)  13.9 us
    another operation x3, other arithmetic, solve_small(): factor = jnp.linalg.cholesky(normal_matrix)  9.45 us
    select_n x4, other arithmetic, on_device(): jnp.take(extended, face_columns, axis=0)  8.94 us
    gather x6, local copies, waits for them, and re-layouts, on_device(): jnp.take(extended, face_columns, axis=0)  8.28 us
    another operation x2, other arithmetic, solve_small(): coeffs = jax.scipy.linalg.cho_solve((factor, True), right_terms)  8.01 us
  transfers between devices with their start and end apart: 14, of which 4 were waited for; matrix products, arithmetic and copies ran while one was open for 3% of the time, Pallas kernels for 0%

profile of v1, /device:TPU:1, one launch (start us, length us, event | category | flops | bytes accessed | tf_op | source)
XLA Modules:
  0.0 378.6 jit_solution(11804494451568773290)
XLA Ops:
  9.6 3.9 %collective-permute-start = (f32[4,2048]{1,0:T(4,128)S(1)}, f32[4,2048]{1,0:T(4,128)S(1)}, u32[]{:S(2)}, u32[]{:S(2)}) collective-permute-start(f32[4,2048]{1,0:T(4,128)S(1)} %broadcast_select_fusion.14), channel_id=1, source_target_pairs={{0,8},{8,16},{16,24},{24,32},{32,40},{40,48},{48,56},{56,64},{64,7... | collective-permute-start | bytes 98312 | tf_op jit(solution)/shard_map/ppermute | solution.py:15
  18.0 4.0 %collective-permute-start.2 = (f32[4,2048]{1,0:T(4,128)S(1)}, f32[4,2048]{1,0:T(4,128)S(1)}, u32[]{:S(2)}, u32[]{:S(2)}) collective-permute-start(f32[4,2048]{1,0:T(4,128)S(1)} %broadcast_select_fusion.12), channel_id=1, source_target_pairs={{0,1},{1,2},{2,3},{3,4},{4,5},{5,6},{6,7},{8,9},{9,10},{10,11},{11... | collective-permute-start | bytes 98312 | tf_op jit(solution)/shard_map/ppermute | solution.py:15
  23.7 1.9 collective-permute-start.3
  27.1 5.7 %reshape.61 = f32[16,11,64,64]{3,2,0,1:T(8,128)} reshape(f32[16,11,4096]{2,0,1:T(8,128)} %param.9) | data formatting | bytes 5767168 | tf_op jit(solution)/shard_map/reshape | solution.py:52
  35.6 1.8 broadcast_select_fusion.2
  37.4 3.6 reshape.245
  41.0 12.0 %fusion.6 = f32[16,64,32]{1,2,0:T(8,128)S(1)} fusion(f32[16,11,64,64]{3,2,0,1:T(8,128)} %reshape.61, f32[16,11,64,32]{3,2,1,0:T(8,128)} %reshape.245), kind=kOutput, calls=%fused_computation.21 | convolution fusion | flops 276824064 | bytes 4456448 | tf_op jit(solution)/shard_map/fkab,fkbr->far/dot_general | solution.py:29
  57.2 3.6 collective-permute-start.6
  60.9 1.9 collective-permute-start.7
  62.9 5.1 %collective-permute-start.4 = (f32[4,2048]{1,0:T(4,128)S(1)}, f32[4,2048]{1,0:T(4,128)S(1)}, u32[]{:S(2)}, u32[]{:S(2)}) collective-permute-start(f32[4,2048]{1,0:T(4,128)S(1)} %broadcast_select_fusion.10), channel_id=1, source_target_pairs={{0,8},{8,16},{16,24},{24,32},{32,40},{40,48},{48,56},{56,64},{64,7... | collective-permute-start | bytes 98312 | tf_op jit(solution)/shard_map/ppermute | solution.py:15
  71.7 3.2 broadcast_select_fusion.1
  74.9 5.2 %reshape.246 = f32[16,11,64,32]{3,2,1,0:T(8,128)} reshape(f32[16,11,2048]{2,1,0:T(8,128)} %broadcast_select_fusion.1) | data formatting | bytes 2883584 | tf_op jit(solution)/shard_map/reshape | solution.py:28
  80.1 12.0 %fusion.9 = f32[16,64,32]{1,2,0:T(8,128)S(1)} fusion(f32[16,11,64,64]{3,2,0,1:T(8,128)} %reshape.61, f32[16,11,64,32]{3,2,1,0:T(8,128)} %reshape.246), kind=kOutput, calls=%fused_computation.22 | convolution fusion | flops 276824064 | bytes 4456448 | tf_op jit(solution)/shard_map/fkab,fkbr->far/dot_general | solution.py:29
  94.9 4.5 %collective-permute-start.10 = (f32[4,2048]{1,0:T(4,128)S(1)}, f32[4,2048]{1,0:T(4,128)S(1)}, u32[]{:S(2)}, u32[]{:S(2)}) collective-permute-start(f32[4,2048]{1,0:T(4,128)S(1)} %broadcast_select_fusion.4), channel_id=1, source_target_pairs={{0,1},{1,2},{2,3},{3,4},{4,5},{5,6},{6,7},{8,9},{9,10},{10,11},{11... | collective-permute-start | bytes 98312 | tf_op jit(solution)/shard_map/ppermute | solution.py:15
  99.5 1.9 collective-permute-start.11
  102.9 4.8 %collective-permute-start.8 = (f32[4,2048]{1,0:T(4,128)S(1)}, f32[4,2048]{1,0:T(4,128)S(1)}, u32[]{:S(2)}, u32[]{:S(2)}) collective-permute-start(f32[4,2048]{1,0:T(4,128)S(1)} %broadcast_select_fusion.6), channel_id=1, source_target_pairs={{0,8},{8,16},{16,24},{24,32},{32,40},{40,48},{48,56},{56,64},{64,7... | collective-permute-start | bytes 98312 | tf_op jit(solution)/shard_map/ppermute | solution.py:15
  111.3 3.2 broadcast_select_fusion
  114.6 5.2 %reshape.247 = f32[16,11,64,32]{3,2,1,0:T(8,128)} reshape(f32[16,11,2048]{2,1,0:T(8,128)} %broadcast_select_fusion) | data formatting | bytes 2883584 | tf_op jit(solution)/shard_map/reshape | solution.py:28
  119.7 12.0 %fusion.12 = f32[16,64,32]{1,2,0:T(8,128)S(1)} fusion(f32[16,11,64,64]{3,2,0,1:T(8,128)} %reshape.61, f32[16,11,64,32]{3,2,1,0:T(8,128)} %reshape.247), kind=kOutput, calls=%fused_computation.23 | convolution fusion | flops 276824064 | bytes 4456448 | tf_op jit(solution)/shard_map/fkab,fkbr->far/dot_general | solution.py:29
  132.4 1.6 fusion.37
  134.4 73.7 %all-reduce.3.cloned.1.call-done = f32[128,128]{1,0:T(8,128)} async-done(((f32[128,128]{1,0:T(8,128)}), f32[128,128]{1,0:T(8,128)}) %all-reduce.3.cloned.1.call-update) | async-done | bytes 65552 | tf_op jit(solution)/shard_map/psum | solution.py:66
  208.1 139.9 %all-reduce.5.cloned.1.call-done = f32[128,128]{1,0:T(8,128)} async-done(((f32[128,128]{1,0:T(8,128)}), f32[128,128]{1,0:T(8,128)}) %all-reduce.5.cloned.1.call-update) | async-done | bytes 65552 | tf_op jit(solution)/shard_map/psum | solution.py:66
  349.4 8.8 %cholesky.16 = f32[96,96]{1,0:T(8,128)S(1)} custom-call(f32[96,96]{1,0:T(8,128)S(1)} %fusion.29), custom_call_target="Cholesky" | custom-call | tf_op jit(solution)/shard_map/jit(cholesky)/cholesky | solution.py:44
  359.5 7.4 %custom-call.10 = f32[1,96,96]{1,2,0:T(8,128)S(1)} custom-call(f32[1,96,96]{2,1,0:T(8,128)S(1)} %fusion.24), custom_call_target="InvertDiagBlocksLowerTriangular" | custom-call | tf_op jit(solution)/shard_map/jit(_cho_solve)/triangular_solve | solution.py:45
  (86 shorter events, 37.2 us)
Async XLA Ops:
  7.2 200.9 %all-reduce.3.cloned.1.call-start = ((), (), s32[]{:S(2)}) async-start(), calls=%async_computation | async-start | bytes 131072 | tf_op jit(solution)/shard_map/psum | solution.py:66
  9.6 23.2 %collective-permute-start = (f32[4,2048]{1,0:T(4,128)S(1)}, f32[4,2048]{1,0:T(4,128)S(1)}, u32[]{:S(2)}, u32[]{:S(2)}) collective-permute-start(f32[4,2048]{1,0:T(4,128)S(1)} %broadcast_select_fusion.14), channel_id=1, source_target_pairs={{0,8},{8,16},{16,24},{24,32},{32,40},{40,48},{48,56},{56,64},{64,7... | collective-permute-start | bytes 98312 | tf_op jit(solution)/shard_map/ppermute | solution.py:15
  15.2 17.6 %collective-permute-start.1 = (f32[4,2048]{1,0:T(4,128)S(1)}, f32[4,2048]{1,0:T(4,128)S(1)}, u32[]{:S(2)}, u32[]{:S(2)}) collective-permute-start(f32[4,2048]{1,0:T(4,128)S(1)} %broadcast_select_fusion.13), channel_id=1, source_target_pairs={{8,0},{16,8},{24,16},{32,24},{40,32},{48,40},{56,48},{64,56},{72,6... | collective-permute-start | bytes 98312 | tf_op jit(solution)/shard_map/ppermute | solution.py:15
  18.0 14.8 %collective-permute-start.2 = (f32[4,2048]{1,0:T(4,128)S(1)}, f32[4,2048]{1,0:T(4,128)S(1)}, u32[]{:S(2)}, u32[]{:S(2)}) collective-permute-start(f32[4,2048]{1,0:T(4,128)S(1)} %broadcast_select_fusion.12), channel_id=1, source_target_pairs={{0,1},{1,2},{2,3},{3,4},{4,5},{5,6},{6,7},{8,9},{9,10},{10,11},{11... | collective-permute-start | bytes 98312 | tf_op jit(solution)/shard_map/ppermute | solution.py:15
  23.7 9.2 %collective-permute-start.3 = (f32[4,2048]{1,0:T(4,128)S(1)}, f32[4,2048]{1,0:T(4,128)S(1)}, u32[]{:S(2)}, u32[]{:S(2)}) collective-permute-start(f32[4,2048]{1,0:T(4,128)S(1)} %broadcast_select_fusion.11), channel_id=1, source_target_pairs={{1,0},{2,1},{3,2},{4,3},{5,4},{6,5},{7,6},{9,8},{10,9},{11,10},{12... | collective-permute-start | bytes 98312 | tf_op jit(solution)/shard_map/ppermute | solution.py:15
  27.1 5.7 %copy-start = (f32[16,2048]{1,0:T(8,128)S(1)}, f32[16,2048]{1,0:T(8,128)}, u32[]{:S(2)}) copy-start(f32[16,2048]{1,0:T(8,128)} %param.8) | copy-start | bytes 393220
  55.8 12.2 %collective-permute-start.5 = (f32[4,2048]{1,0:T(4,128)S(1)}, f32[4,2048]{1,0:T(4,128)S(1)}, u32[]{:S(2)}, u32[]{:S(2)}) collective-permute-start(f32[4,2048]{1,0:T(4,128)S(1)} %broadcast_select_fusion.9), channel_id=1, source_target_pairs={{8,0},{16,8},{24,16},{32,24},{40,32},{48,40},{56,48},{64,56},{72,6... | collective-permute-start | bytes 98312 | tf_op jit(solution)/shard_map/ppermute | solution.py:15
  57.2 10.8 %collective-permute-start.6 = (f32[4,2048]{1,0:T(4,128)S(1)}, f32[4,2048]{1,0:T(4,128)S(1)}, u32[]{:S(2)}, u32[]{:S(2)}) collective-permute-start(f32[4,2048]{1,0:T(4,128)S(1)} %broadcast_select_fusion.8), channel_id=1, source_target_pairs={{0,1},{1,2},{2,3},{3,4},{4,5},{5,6},{6,7},{8,9},{9,10},{10,11},{11... | collective-permute-start | bytes 98312 | tf_op jit(solution)/shard_map/ppermute | solution.py:15
  60.9 7.1 %collective-permute-start.7 = (f32[4,2048]{1,0:T(4,128)S(1)}, f32[4,2048]{1,0:T(4,128)S(1)}, u32[]{:S(2)}, u32[]{:S(2)}) collective-permute-start(f32[4,2048]{1,0:T(4,128)S(1)} %broadcast_select_fusion.7), channel_id=1, source_target_pairs={{1,0},{2,1},{3,2},{4,3},{5,4},{6,5},{7,6},{9,8},{10,9},{11,10},{12... | collective-permute-start | bytes 98312 | tf_op jit(solution)/shard_map/ppermute | solution.py:15
  62.9 5.9 %collective-permute-start.4 = (f32[4,2048]{1,0:T(4,128)S(1)}, f32[4,2048]{1,0:T(4,128)S(1)}, u32[]{:S(2)}, u32[]{:S(2)}) collective-permute-start(f32[4,2048]{1,0:T(4,128)S(1)} %broadcast_select_fusion.10), channel_id=1, source_target_pairs={{0,8},{8,16},{16,24},{24,32},{32,40},{40,48},{48,56},{56,64},{64,7... | collective-permute-start | bytes 98312 | tf_op jit(solution)/shard_map/ppermute | solution.py:15
  94.9 12.9 %collective-permute-start.10 = (f32[4,2048]{1,0:T(4,128)S(1)}, f32[4,2048]{1,0:T(4,128)S(1)}, u32[]{:S(2)}, u32[]{:S(2)}) collective-permute-start(f32[4,2048]{1,0:T(4,128)S(1)} %broadcast_select_fusion.4), channel_id=1, source_target_pairs={{0,1},{1,2},{2,3},{3,4},{4,5},{5,6},{6,7},{8,9},{9,10},{10,11},{11... | collective-permute-start | bytes 98312 | tf_op jit(solution)/shard_map/ppermute | solution.py:15
  99.5 8.3 %collective-permute-start.11 = (f32[4,2048]{1,0:T(4,128)S(1)}, f32[4,2048]{1,0:T(4,128)S(1)}, u32[]{:S(2)}, u32[]{:S(2)}) collective-permute-start(f32[4,2048]{1,0:T(4,128)S(1)} %broadcast_select_fusion.3), channel_id=1, source_target_pairs={{1,0},{2,1},{3,2},{4,3},{5,4},{6,5},{7,6},{9,8},{10,9},{11,10},{12... | collective-permute-start | bytes 98312 | tf_op jit(solution)/shard_map/ppermute | solution.py:15
  101.5 6.3 %collective-permute-start.9 = (f32[4,2048]{1,0:T(4,128)S(1)}, f32[4,2048]{1,0:T(4,128)S(1)}, u32[]{:S(2)}, u32[]{:S(2)}) collective-permute-start(f32[4,2048]{1,0:T(4,128)S(1)} %broadcast_select_fusion.5), channel_id=1, source_target_pairs={{8,0},{16,8},{24,16},{32,24},{40,32},{48,40},{56,48},{64,56},{72,6... | collective-permute-start | bytes 98312 | tf_op jit(solution)/shard_map/ppermute | solution.py:15
  102.9 5.6 %collective-permute-start.8 = (f32[4,2048]{1,0:T(4,128)S(1)}, f32[4,2048]{1,0:T(4,128)S(1)}, u32[]{:S(2)}, u32[]{:S(2)}) collective-permute-start(f32[4,2048]{1,0:T(4,128)S(1)} %broadcast_select_fusion.6), channel_id=1, source_target_pairs={{0,8},{8,16},{16,24},{24,32},{32,40},{40,48},{48,56},{56,64},{64,7... | collective-permute-start | bytes 98312 | tf_op jit(solution)/shard_map/ppermute | solution.py:15
  134.1 213.9 %all-reduce.5.cloned.1.call-start = ((), (), s32[]{:S(2)}) async-start(), calls=%async_computation.1 | async-start | bytes 131072 | tf_op jit(solution)/shard_map/psum | solution.py:66
Sparse Core Ops, SparseCore 0:
  134.2 73.8 all-reduce.2
  211.9 136.0 all-reduce.4
